TPU v7x, 256 devices: a whole 4x4x8 slice. The times are simulated.
256 devices in a mesh: seq: 32 (over y, z), grp: 8 (over x, core).
Axes of the slice: x: 4, y: 4, z: 8, core: 2. Of those that a mesh axis runs over, the one named last changes fastest.
Arguments:
- hidden: bfloat16 [16384, 2048], P('seq', 'grp'), may hold values from -8 to 8
- qkv_weight: bfloat16 [3, 2048, 6144], P(None, 'seq', 'grp'), may hold values from -0.125 to 0.125
- out_weight: bfloat16 [3, 2048, 2048], P(None, 'grp', 'seq'), may hold values from -0.125 to 0.125
- projection: float32 [3, 16, 128, 128], P(None, 'grp'), may hold values from -6 to 6
- norm_gain: float32 [3, 2048], replicated, may hold values from 0.1 to 1.9
- out_gain: float32 [3, 2048], P(None, 'grp'), may hold values from 0.1 to 1.9
Outputs:
- layer_out: bfloat16 [16384, 2048], P('seq', 'grp')
All inputs are finite; a program needn't handle non-finite values.
Results may differ from a plain program's by a relative error of at most 0.034.
Values may be sent and summed in bfloat16 or wider, within the bound.
No kernel may reach another device: no remote copies, remote signals or barrier semaphores. Data moves between devices by JAX's collectives and lax.ppermute only.
A program may use at most 64 MiB of HBM per device.

v0:
```python
import math
import jax
import jax.numpy as jnp
from jax import lax
from jax.sharding import Mesh
from jax.sharding import PartitionSpec as P

SEQ = ("seq_0", "seq_1")
stabilizer = 2.0
highest = lax.Precision.HIGHEST


def sent_to_all(array, axis):
    peers = lax.axis_size(axis)
    return lax.all_to_all(
        jnp.broadcast_to(array[None], (peers, *array.shape)), axis, 0, 0, tiled=True
    )


def joined_along(tiles, dim):
    lengths = list(tiles.shape[1:])
    lengths[dim] *= tiles.shape[0]
    return jnp.moveaxis(tiles, 0, dim).reshape(lengths)


def gathered_copies(array, axis, dim):
    tiles = sent_to_all(array, axis)
    return joined_along(tiles, dim)


def neutral_like(array, identity):
    return jax.tree.map(
        lambda a, e: jnp.broadcast_to(jnp.asarray(e, a.dtype), a.shape), array, identity
    )


def entering(array, axes, combine, identity):
    before = start = neutral_like(array, identity)
    subtotal = array
    for axis in reversed(axes):
        peers, index = (lax.axis_size(axis), lax.axis_index(axis))
        pieces = jax.tree.map(
            lambda part, kind: lax.all_gather(part.astype(kind), axis),
            subtotal,
            (jnp.bfloat16, jnp.bfloat16),
        )
        inside, subtotal = (start, start)
        for k in range(peers):
            passed = k < index
            subtotal = combine(
                subtotal, jax.tree.map(lambda part, own: part[k].astype(own.dtype), pieces, array)
            )
            inside = jax.tree.map(lambda new, old: jnp.where(passed, new, old), subtotal, inside)
        before = combine(inside, before)
    return before


def in_blocks(array, dim, peers):
    lengths = array.shape
    tiles = array.reshape(*lengths[:dim], peers, lengths[dim] // peers, *lengths[dim + 1 :])
    return jnp.moveaxis(tiles, dim, 0)


def sum_at_owner(array, axis, dim):
    tiles = in_blocks(array, dim, lax.axis_size(axis))
    arrived = lax.all_to_all(tiles, axis, split_axis=0, concat_axis=0, tiled=True)
    return arrived.astype(jnp.float32).sum(axis=0)


def features(rows, projection_layer):
    head_size = rows.shape[-1]
    feature_count = projection_layer.shape[-1]
    scaled = rows.astype(jnp.float32) * head_size ** (-0.25)
    mixed = jnp.einsum("thd,hdm->thm", scaled, projection_layer, precision=highest)
    energy = 0.5 * jnp.sum(scaled * scaled, axis=-1, keepdims=True)
    return (jnp.exp(mixed - energy - stabilizer) / math.sqrt(feature_count)).astype(jnp.bfloat16)


def add_states(earlier, later):
    return (earlier[0] + later[0], earlier[1] + later[1])


def local(hidden, qkv_weight, out_weight, projection, norm_gain, out_gain):
    layer_count = qkv_weight.shape[0]
    local_heads = projection.shape[1]
    head_size = projection.shape[2]
    feature_count = projection.shape[3]
    token_rows = hidden.shape[0]
    stream = hidden
    causal_mask = jnp.arange(token_rows)[:, None] >= jnp.arange(token_rows)[None, :]
    for layer_index in range(layer_count):
        gathered = gathered_copies(stream, "grp", 1)
        wide = gathered.astype(jnp.float32)
        inverse_rms = lax.rsqrt(jnp.mean(wide * wide, axis=-1, keepdims=True) + 1e-05)
        normed = (wide * inverse_rms * norm_gain[layer_index][None, :]).astype(jnp.bfloat16)
        qkv_wide = jnp.dot(
            normed,
            lax.all_gather(qkv_weight[layer_index], SEQ, axis=0, tiled=True),
            preferred_element_type=jnp.float32,
        )
        qkv = qkv_wide.astype(jnp.bfloat16).reshape(token_rows, local_heads, 3, head_size)
        query_feat = features(qkv[:, :, 0], projection[layer_index])
        key_feat = features(qkv[:, :, 1], projection[layer_index])
        value_rows = qkv[:, :, 2]
        block_kv = jnp.einsum(
            "jhm,jhe->hme", key_feat, value_rows, preferred_element_type=jnp.float32
        )
        block_z = jnp.sum(key_feat.astype(jnp.float32), axis=0)
        zero_kv = jnp.zeros((local_heads, feature_count, head_size), jnp.float32)
        zero_z = jnp.zeros((local_heads, feature_count), jnp.float32)
        prefix_kv, prefix_z = entering((block_kv, block_z), SEQ, add_states, (zero_kv, zero_z))
        scores = jnp.einsum(
            "ihm,jhm->hij", query_feat, key_feat, preferred_element_type=jnp.float32
        )
        masked = jnp.where(causal_mask[None], scores, jnp.zeros_like(scores))
        score_weights = masked.astype(jnp.bfloat16)
        query_wide = query_feat.astype(jnp.float32)
        denominator = jnp.sum(masked, axis=-1) + jnp.einsum(
            "ihm,hm->hi", query_wide, prefix_z, precision=highest
        )
        numerator = jnp.einsum(
            "hij,jhe->hie", score_weights, value_rows, preferred_element_type=jnp.float32
        )
        numerator = numerator + jnp.einsum(
            "ihm,hme->hie",
            query_feat,
            prefix_kv.astype(jnp.bfloat16),
            preferred_element_type=jnp.float32,
        )
        attention = numerator / denominator[..., None]
        inverse_norm = lax.rsqrt(jnp.mean(attention * attention, axis=-1, keepdims=True) + 1e-06)
        head_gain = out_gain[layer_index].reshape(local_heads, head_size)[:, None, :]
        attended = (attention * inverse_norm * head_gain).astype(jnp.bfloat16)
        attended = jnp.transpose(attended, (1, 0, 2)).reshape(token_rows, local_heads * head_size)
        terms = jnp.dot(
            attended,
            gathered_copies(out_weight[layer_index], SEQ, 1),
            preferred_element_type=jnp.float32,
        )
        summed = sum_at_owner(terms.astype(jnp.bfloat16), "grp", 1)
        stream = (stream.astype(jnp.float32) + summed).astype(jnp.bfloat16)
    return stream


def solution(mesh):
    finer = Mesh(mesh.devices.reshape(4, 8, mesh.shape["grp"]), ("seq_0", "seq_1", "grp"))
    in_specs = (
        P(SEQ, "grp"),
        P(None, SEQ, "grp"),
        P(None, "grp", SEQ),
        P(None, "grp", None, None),
        P(),
        P(None, "grp"),
    )
    out_specs = P(SEQ, "grp")
    return jax.shard_map(local, mesh=finer, in_specs=in_specs, out_specs=out_specs, check_vma=False)
```

profile of v0, /device:TPU:1, one launch (start us, length us, event | category | flops | bytes accessed | tf_op | source)
XLA Modules:
  0.0 526.0 jit_solution(9621818431269840428)
XLA Ops:
  6.5 1.7 fusion.264
  8.3 1.1 copy.52
  9.4 1.5 broadcast_in_dim.37
  10.9 6.9 %all-to-all-start = ((bf16[8,512,256]{1,2,0:T(8,128)(2,1)}), bf16[8,512,256]{1,2,0:T(8,128)(2,1)S(1)}, u32[]{:S(2)}, u32[]{:S(2)}) async-start(bf16[8,512,256]{1,2,0:T(8,128)(2,1)} %broadcast_in_dim.37), calls=%async_computation | async-start | bytes 4194304 | tf_op jit(solution)/shard_map/all_to_all | solution.py:15
  17.8 0.7 all-gather.18.cloned.1.call-update
  18.7 25.4 %all-to-all-done = bf16[8,512,256]{1,2,0:T(8,128)(2,1)S(1)} async-done(((bf16[8,512,256]{1,2,0:T(8,128)(2,1)}), bf16[8,512,256]{1,2,0:T(8,128)(2,1)S(1)}, u32[]{:S(2)}, u32[]{:S(2)}) %all-to-all-start) | async-done | bytes 2097184 | tf_op jit(solution)/shard_map/all_to_all | solution.py:15
  44.1 1.2 broadcast_in_dim.39
  45.3 10.2 %all-to-all-start.1 = ((bf16[32,256,64]{1,2,0:T(8,128)(2,1)}), bf16[32,256,64]{1,2,0:T(8,128)(2,1)S(1)}, u32[]{:S(2)}, u32[]{:S(2)}) async-start(bf16[32,256,64]{1,2,0:T(8,128)(2,1)} %broadcast_in_dim.39), calls=%async_computation.1 | async-start | bytes 2097152 | tf_op jit(solution)/shard_map/all_to_all | solution.py:15
  56.1 1.9 fusion.5
  58.0 42.3 %all-gather.16.cloned.1.call-done = bf16[1,2048,768]{2,1,0:T(8,128)(2,1)} async-done(((bf16[1,64,768]{2,1,0:T(8,128)(2,1)}), bf16[1,2048,768]{2,1,0:T(8,128)(2,1)}) %all-gather.16.cloned.1.call-update) | async-done | bytes 3145744 | tf_op jit(solution)/shard_map/all_gather | solution.py:98
  100.3 4.4 fusion.12
  105.9 0.7 fusion.50
  106.5 0.7 fusion.267
  107.2 10.7 %all-gather.9 = bf16[8,2,128]{2,1,0:T(2,128)(2,1)S(1)} all-gather(bf16[1,2,128]{2,1,0:T(2,128)(2,1)S(1)} %bitcast.627), channel_id=4, replica_groups=mesh['seq_0'=4,'seq_1'=8,'grp'=8] {'seq_1'}, dimensions={0}, use_global_device_ids=true | all-gather | bytes 4608 | tf_op jit(solution)/shard_map/all_gather | solution.py:43
  118.0 8.1 %all_gather.75 = bf16[4,2,128]{2,1,0:T(2,128)(2,1)S(1)} all-gather(bf16[1,2,128]{2,1,0:T(2,128)(2,1)S(1)} %fusion.246), channel_id=1, replica_groups=mesh['seq_0'=4,'seq_1'=8,'grp'=8] {'seq_0'}, dimensions={0}, use_global_device_ids=true | all-gather | bytes 2560 | tf_op jit(solution)/shard_map/all_gather | solution.py:43
  126.7 20.7 %all-gather.1 = bf16[16,128,128]{2,1,0:T(8,128)(2,1)S(1)} all-gather(bf16[2,128,128]{2,1,0:T(8,128)(2,1)S(1)} %convolution_convert_fusion.5), channel_id=3, replica_groups=mesh['seq_0'=4,'seq_1'=8,'grp'=8] {'seq_1'}, dimensions={0}, use_global_device_ids=true | all-gather | bytes 589824 | tf_op jit(solution)/shard_map/all_gather | solution.py:43
  147.5 10.9 %all_gather.72 = bf16[4,2,128,128]{3,2,1,0:T(8,128)(2,1)S(1)} all-gather(bf16[1,2,128,128]{3,2,1,0:T(8,128)(2,1)S(1)} %fusion.125), channel_id=1, replica_groups=mesh['seq_0'=4,'seq_1'=8,'grp'=8] {'seq_0'}, dimensions={0}, use_global_device_ids=true | all-gather | bytes 327680 | tf_op jit(solution)/shard_map/all_gather | solution.py:43
  159.8 0.8 convolution_convert_fusion.2
  160.7 44.9 %all_to_all.45 = bf16[8,512,256]{2,1,0:T(8,128)(2,1)S(1)} all-to-all(bf16[8,512,256]{2,1,0:T(8,128)(2,1)S(1)} %bitcast.597), channel_id=1, replica_groups=mesh['seq_0'=4,'seq_1'=8,'grp'=8] {'grp'}, dimensions={0} | all-to-all | bytes 4194304 | tf_op jit(solution)/shard_map/all_to_all | solution.py:66
  206.8 1.5 broadcast_in_dim.40
  208.3 4.5 all-to-all-start.3
  212.9 0.7 all-gather.20.cloned.1.call-update
  213.6 25.6 %all-to-all-done.3 = bf16[8,512,256]{1,2,0:T(8,128)(2,1)S(1)} async-done(((bf16[8,512,256]{1,2,0:T(8,128)(2,1)}), bf16[8,512,256]{1,2,0:T(8,128)(2,1)S(1)}, u32[]{:S(2)}, u32[]{:S(2)}) %all-to-all-start.3) | async-done | bytes 2097184 | tf_op jit(solution)/shard_map/all_to_all | solution.py:15
  239.2 1.2 broadcast_in_dim.42
  240.4 5.0 all-to-all-start.4
  245.9 1.9 fusion.3
  247.8 4.4 fusion.15
  253.4 1.7 fusion.268
  255.0 23.2 %all-gather.10 = bf16[8,2,128]{2,1,0:T(2,128)(2,1)S(1)} all-gather(bf16[1,2,128]{2,1,0:T(2,128)(2,1)S(1)} %bitcast.628), channel_id=7, replica_groups=mesh['seq_0'=4,'seq_1'=8,'grp'=8] {'seq_1'}, dimensions={0}, use_global_device_ids=true | all-gather | bytes 4608 | tf_op jit(solution)/shard_map/all_gather | solution.py:43
  278.3 8.0 %all_gather.82 = bf16[4,2,128]{2,1,0:T(2,128)(2,1)S(1)} all-gather(bf16[1,2,128]{2,1,0:T(2,128)(2,1)S(1)} %fusion.247), channel_id=1, replica_groups=mesh['seq_0'=4,'seq_1'=8,'grp'=8] {'seq_0'}, dimensions={0}, use_global_device_ids=true | all-gather | bytes 2560 | tf_op jit(solution)/shard_map/all_gather | solution.py:43
  286.5 21.1 %all-gather.4 = bf16[16,128,128]{2,1,0:T(8,128)(2,1)S(1)} all-gather(bf16[2,128,128]{2,1,0:T(8,128)(2,1)S(1)} %convolution_convert_fusion.4), channel_id=6, replica_groups=mesh['seq_0'=4,'seq_1'=8,'grp'=8] {'seq_1'}, dimensions={0}, use_global_device_ids=true | all-gather | bytes 589824 | tf_op jit(solution)/shard_map/all_gather | solution.py:43
  307.7 9.4 %all_gather.79 = bf16[4,2,128,128]{3,2,1,0:T(8,128)(2,1)S(1)} all-gather(bf16[1,2,128,128]{3,2,1,0:T(8,128)(2,1)S(1)} %fusion.124), channel_id=1, replica_groups=mesh['seq_0'=4,'seq_1'=8,'grp'=8] {'seq_0'}, dimensions={0}, use_global_device_ids=true | all-gather | bytes 327680 | tf_op jit(solution)/shard_map/all_gather | solution.py:43
  317.0 1.6 fusion.48
  320.4 0.8 convolution_convert_fusion.1
  321.3 42.6 %all_to_all.46 = bf16[8,512,256]{2,1,0:T(8,128)(2,1)S(1)} all-to-all(bf16[8,512,256]{2,1,0:T(8,128)(2,1)S(1)} %bitcast.598), channel_id=1, replica_groups=mesh['seq_0'=4,'seq_1'=8,'grp'=8] {'grp'}, dimensions={0} | all-to-all | bytes 4194304 | tf_op jit(solution)/shard_map/all_to_all | solution.py:66
  364.7 30.0 %all_to_all.47 = bf16[8,512,256]{1,2,0:T(8,128)(2,1)S(1)} all-to-all(bf16[8,512,256]{1,2,0:T(8,128)(2,1)S(1)} %broadcast_in_dim.43), channel_id=1, replica_groups=mesh['seq_0'=4,'seq_1'=8,'grp'=8] {'grp'}, dimensions={0} | all-to-all | bytes 4194304 | tf_op jit(solution)/shard_map/all_to_all | solution.py:15
  394.6 1.1 broadcast_in_dim.45
  395.7 6.9 %all-to-all-start.7 = ((bf16[32,256,64]{1,2,0:T(8,128)(2,1)}), bf16[32,256,64]{1,2,0:T(8,128)(2,1)S(1)}, u32[]{:S(2)}, u32[]{:S(2)}) async-start(bf16[32,256,64]{1,2,0:T(8,128)(2,1)} %broadcast_in_dim.45), calls=%async_computation.7 | async-start | bytes 2097152 | tf_op jit(solution)/shard_map/all_to_all | solution.py:15
  403.1 1.9 fusion.1
  405.0 4.4 fusion.18
  410.6 0.7 fusion.269
  411.3 21.4 %all-gather.11 = bf16[8,2,128]{2,1,0:T(2,128)(2,1)S(1)} all-gather(bf16[1,2,128]{2,1,0:T(2,128)(2,1)S(1)} %bitcast.629), channel_id=10, replica_groups=mesh['seq_0'=4,'seq_1'=8,'grp'=8] {'seq_1'}, dimensions={0}, use_global_device_ids=true | all-gather | bytes 4608 | tf_op jit(solution)/shard_map/all_gather | solution.py:43
  432.7 7.6 %all_gather.89 = bf16[4,2,128]{2,1,0:T(2,128)(2,1)S(1)} all-gather(bf16[1,2,128]{2,1,0:T(2,128)(2,1)S(1)} %fusion.248), channel_id=1, replica_groups=mesh['seq_0'=4,'seq_1'=8,'grp'=8] {'seq_0'}, dimensions={0}, use_global_device_ids=true | all-gather | bytes 2560 | tf_op jit(solution)/shard_map/all_gather | solution.py:43
  440.6 19.7 %all-gather.7 = bf16[16,128,128]{2,1,0:T(8,128)(2,1)S(1)} all-gather(bf16[2,128,128]{2,1,0:T(8,128)(2,1)S(1)} %convolution_convert_fusion.3), channel_id=9, replica_groups=mesh['seq_0'=4,'seq_1'=8,'grp'=8] {'seq_1'}, dimensions={0}, use_global_device_ids=true | all-gather | bytes 589824 | tf_op jit(solution)/shard_map/all_gather | solution.py:43
  460.4 9.4 %all_gather.86 = bf16[4,2,128,128]{3,2,1,0:T(8,128)(2,1)S(1)} all-gather(bf16[1,2,128,128]{3,2,1,0:T(8,128)(2,1)S(1)} %fusion.123), channel_id=1, replica_groups=mesh['seq_0'=4,'seq_1'=8,'grp'=8] {'seq_0'}, dimensions={0}, use_global_device_ids=true | all-gather | bytes 327680 | tf_op jit(solution)/shard_map/all_gather | solution.py:43
  472.3 0.8 convolution_convert_fusion
  473.2 44.6 %all_to_all.48 = bf16[8,512,256]{2,1,0:T(8,128)(2,1)S(1)} all-to-all(bf16[8,512,256]{2,1,0:T(8,128)(2,1)S(1)} %bitcast.599), channel_id=1, replica_groups=mesh['seq_0'=4,'seq_1'=8,'grp'=8] {'grp'}, dimensions={0} | all-to-all | bytes 4194304 | tf_op jit(solution)/shard_map/all_to_all | solution.py:66
  518.7 0.8 add_convert_fusion
  (110 shorter events, 15.2 us)
Async XLA Ops:
  6.5 93.8 %all-gather.16.cloned.1.call-start = ((), (), s32[]{:S(2)}) async-start(), calls=%async_computation.9 | async-start | bytes 3244032 | tf_op jit(solution)/shard_map/all_gather | solution.py:98
  10.9 7.7 %copy-start.8 = (f32[3,256]{1,0:T(4,128)S(1)}, f32[3,256]{1,0:T(4,128)}, u32[]{:S(2)}) copy-start(f32[3,256]{1,0:T(4,128)} %param.11) | copy-start | bytes 9220
  10.9 7.8 %copy-start.6 = (bf16[3,256,64]{1,2,0:T(8,128)(2,1)S(1)}, bf16[3,256,64]{1,2,0:T(8,128)(2,1)}, u32[]{:S(2)}) copy-start(bf16[3,256,64]{1,2,0:T(8,128)(2,1)} %param.8) | copy-start | bytes 294916
  10.9 7.8 %copy-start.7 = (f32[3,2048]{1,0:T(4,128)S(1)}, f32[3,2048]{1,0:T(4,128)}, u32[]{:S(2)}) copy-start(f32[3,2048]{1,0:T(4,128)} %param.10) | copy-start | bytes 73732
  10.9 33.2 %all-to-all-start = ((bf16[8,512,256]{1,2,0:T(8,128)(2,1)}), bf16[8,512,256]{1,2,0:T(8,128)(2,1)S(1)}, u32[]{:S(2)}, u32[]{:S(2)}) async-start(bf16[8,512,256]{1,2,0:T(8,128)(2,1)} %broadcast_in_dim.37), calls=%async_computation | async-start | bytes 4194304 | tf_op jit(solution)/shard_map/all_to_all | solution.py:15
  17.8 230.0 %all-gather.18.cloned.1.call-start = ((), (), s32[]{:S(2)}) async-start(), calls=%async_computation.10 | async-start | bytes 3244032 | tf_op jit(solution)/shard_map/all_gather | solution.py:98
  18.6 140.6 %copy-start.3 = (pred[512,512]{0,1:T(8,128)(4,1)}, pred[512,512]{0,1:T(8,128)(4,1)S(1)}, u32[]{:S(2)}) copy-start(pred[512,512]{0,1:T(8,128)(4,1)S(1)} %iota_compare_fusion) | copy-start | bytes 786436
  45.3 114.5 %all-to-all-start.1 = ((bf16[32,256,64]{1,2,0:T(8,128)(2,1)}), bf16[32,256,64]{1,2,0:T(8,128)(2,1)S(1)}, u32[]{:S(2)}, u32[]{:S(2)}) async-start(bf16[32,256,64]{1,2,0:T(8,128)(2,1)} %broadcast_in_dim.39), calls=%async_computation.1 | async-start | bytes 2097152 | tf_op jit(solution)/shard_map/all_to_all | solution.py:15
  104.7 1.2 copy-start.9
  205.7 1.0 copy-start.2
  208.3 30.9 %all-to-all-start.3 = ((bf16[8,512,256]{1,2,0:T(8,128)(2,1)}), bf16[8,512,256]{1,2,0:T(8,128)(2,1)S(1)}, u32[]{:S(2)}, u32[]{:S(2)}) async-start(bf16[8,512,256]{1,2,0:T(8,128)(2,1)} %broadcast_in_dim.40), calls=%async_computation.3 | async-start | bytes 4194304 | tf_op jit(solution)/shard_map/all_to_all | solution.py:15
  212.9 192.1 %all-gather.20.cloned.1.call-start = ((), (), s32[]{:S(2)}) async-start(), calls=%async_computation.11 | async-start | bytes 3244032 | tf_op jit(solution)/shard_map/all_gather | solution.py:98
  240.4 80.0 %all-to-all-start.4 = ((bf16[32,256,64]{1,2,0:T(8,128)(2,1)}), bf16[32,256,64]{1,2,0:T(8,128)(2,1)S(1)}, u32[]{:S(2)}, u32[]{:S(2)}) async-start(bf16[32,256,64]{1,2,0:T(8,128)(2,1)} %broadcast_in_dim.42), calls=%async_computation.4 | async-start | bytes 2097152 | tf_op jit(solution)/shard_map/all_to_all | solution.py:15
  253.3 65.6 %copy-start.4 = (pred[512,512]{0,1:T(8,128)(4,1)S(1)}, pred[512,512]{0,1:T(8,128)(4,1)}, u32[]{:S(2)}) copy-start(pred[512,512]{0,1:T(8,128)(4,1)} %copy-done.3) | copy-start | bytes 786436
  364.3 30.3 %copy-start = (bf16[512,256]{1,0:T(8,128)(2,1)}, bf16[512,256]{1,0:T(8,128)(2,1)S(1)}, u32[]{:S(2)}) copy-start(bf16[512,256]{1,0:T(8,128)(2,1)S(1)} %add_convert_fusion.1) | copy-start | bytes 786436
  395.7 76.6 %all-to-all-start.7 = ((bf16[32,256,64]{1,2,0:T(8,128)(2,1)}), bf16[32,256,64]{1,2,0:T(8,128)(2,1)S(1)}, u32[]{:S(2)}, u32[]{:S(2)}) async-start(bf16[32,256,64]{1,2,0:T(8,128)(2,1)} %broadcast_in_dim.45), calls=%async_computation.7 | async-start | bytes 2097152 | tf_op jit(solution)/shard_map/all_to_all | solution.py:15
  409.4 1.2 copy-start.10
  410.6 60.2 %copy-start.5 = (pred[512,512]{0,1:T(8,128)(4,1)S(1)}, pred[512,512]{0,1:T(8,128)(4,1)}, u32[]{:S(2)}) copy-start(pred[512,512]{0,1:T(8,128)(4,1)} %copy-done.3) | copy-start | bytes 786436
  517.8 1.0 copy-start.1
Sparse Core Ops, SparseCore 0:
  9.9 90.3 all-gather.15
  102.9 75.2 all-gather.17
  216.3 77.1 all-gather.19
where the time goes:
time: 527 us; the launch traced here: 526 us
  blocking collectives  332 us (63%)
  waiting for transfers between devices  94.8 us (18%)
  starting transfers between devices  33.5 us (6%)
  matrix products  27 us (5%)
  between operations  13.7 us (3%)
  local copies, waits for them, and re-layouts  13.5 us (3%)
  other arithmetic  11.1 us (2%)
    all_gather x12, blocking collectives, entering(): lax.all_gather(part.astype(kind), axis)  170 us
    all_to_all x3, blocking collectives, sum_at_owner(): lax.all_to_all(tiles, axis, split_axis=0, concat_axis=0, tiled=True)  132 us
    all_to_all x5, waiting for transfers between devices, sent_to_all(): lax.all_to_all(jnp.broadcast_to(array[None], (peers, *array.shape)), axis...  51 us
    all_gather x3, waiting for transfers between devices, local(): lax.all_gather(qkv_weight[layer_index], SEQ, axis=0, tiled=True)  42.3 us
    all_to_all x5, starting transfers between devices, sent_to_all(): lax.all_to_all(jnp.broadcast_to(array[None], (peers, *array.shape)), axis...  33.5 us
    all_to_all x1, blocking collectives, sent_to_all(): lax.all_to_all(jnp.broadcast_to(array[None], (peers, *array.shape)), axis...  30 us
    dot_general x3, matrix products, local(): jnp.dot(normed, lax.all_gather(qkv_weight[layer_index], SEQ, axis=0, tile...  13.1 us
  transfers between devices with their start and end apart: 8, of which 3 were waited for; matrix products, arithmetic and copies ran while one was open for 9% of the time, Pallas kernels for 0%

commit v1 on v0

--- a/solution.py
+++ b/solution.py
@@ -95,7 +95,12 @@
         normed = (wide * inverse_rms * norm_gain[layer_index][None, :]).astype(jnp.bfloat16)
         qkv_wide = jnp.dot(
             normed,
-            lax.all_gather(qkv_weight[layer_index], SEQ, axis=0, tiled=True),
+            jnp.concatenate(
+                lax.all_to_all(
+                    jnp.stack([qkv_weight[layer_index]] * lax.axis_size(SEQ)), SEQ, 0, 0
+                ),
+                axis=0,
+            ),
             preferred_element_type=jnp.float32,
         )
         qkv = qkv_wide.astype(jnp.bfloat16).reshape(token_rows, local_heads, 3, head_size)

time: 527 us -> 726 us (1.38)
  waiting for transfers between devices: 94.8 us -> 231 us
  blocking collectives: 332 us -> 374 us
  starting transfers between devices: 33.5 us -> 56.5 us
  between operations: 13.7 us -> 0.66 us
    all_to_all x0 -> x3, waiting for transfers between devices: none -> 205 us  [local(): lax.all_to_all(jnp.stack([qkv_weight[layer_index]] * lax.axis_size(SEQ)),...]
    all_gather x3 -> x0, waiting for transfers between devices: 42.3 us -> none  [local(): lax.all_gather(qkv_weight[layer_index], SEQ, axis=0, tiled=True)]
    all_to_all x1 -> x2, blocking collectives: 30 us -> 59.9 us  [sent_to_all(): lax.all_to_all(jnp.broadcast_to(array[None], (peers, *array.shape)), axis...]
    all_to_all x5 -> x4, waiting for transfers between devices: 51 us -> 26.3 us  [sent_to_all(): lax.all_to_all(jnp.broadcast_to(array[None], (peers, *array.shape)), axis...]
    all_to_all x0 -> x3, starting transfers between devices: none -> 24.3 us  [local(): lax.all_to_all(jnp.stack([qkv_weight[layer_index]] * lax.axis_size(SEQ)),...]
    all_gather x12, blocking collectives: 170 us -> 179 us  [entering(): lax.all_gather(part.astype(kind), axis)]
    all_to_all x5 -> x4, starting transfers between devices: 33.5 us -> 32.3 us  [sent_to_all(): lax.all_to_all(jnp.broadcast_to(array[None], (peers, *array.shape)), axis...]
  transfers between devices with their start and end apart: 8 -> 7, of which waited for: 3 -> 4; matrix products, arithmetic and copies ran while one was open for 9% -> 6% of each run, Pallas kernels for 0% -> 0%
where the time goes in v1:
time: 726 us; the launch traced here: 725 us
  blocking collectives  374 us (52%)
  waiting for transfers between devices  231 us (32%)
  starting transfers between devices  56.5 us (8%)
  matrix products  32.9 us (5%)
  local copies, waits for them, and re-layouts  18.4 us (3%)
  other arithmetic  11.8 us (2%)
    all_to_all x3, waiting for transfers between devices, local(): lax.all_to_all(jnp.stack([qkv_weight[layer_index]] * lax.axis_size(SEQ)),...  205 us
    all_gather x12, blocking collectives, entering(): lax.all_gather(part.astype(kind), axis)  179 us
    all_to_all x3, blocking collectives, sum_at_owner(): lax.all_to_all(tiles, axis, split_axis=0, concat_axis=0, tiled=True)  135 us
    all_to_all x2, blocking collectives, sent_to_all(): lax.all_to_all(jnp.broadcast_to(array[None], (peers, *array.shape)), axis...  59.9 us
    all_to_all x4, starting transfers between devices, sent_to_all(): lax.all_to_all(jnp.broadcast_to(array[None], (peers, *array.shape)), axis...  32.3 us
    all_to_all x4, waiting for transfers between devices, sent_to_all(): lax.all_to_all(jnp.broadcast_to(array[None], (peers, *array.shape)), axis...  26.3 us
    all_to_all x3, starting transfers between devices, local(): lax.all_to_all(jnp.stack([qkv_weight[layer_index]] * lax.axis_size(SEQ)),...  24.3 us
  transfers between devices with their start and end apart: 7, of which 4 were waited for; matrix products, arithmetic and copies ran while one was open for 6% of the time, Pallas kernels for 0%

profile of v1, /device:TPU:1, one launch (start us, length us, event | category | flops | bytes accessed | tf_op | source)
XLA Modules:
  0.0 725.1 jit_solution(15657649643887399041)
XLA Ops:
  1.1 1.5 broadcast_in_dim.37
  2.6 6.9 all-to-all-start
  9.5 26.3 %all-to-all-done = bf16[8,512,256]{1,2,0:T(8,128)(2,1)S(1)} async-done(((bf16[8,512,256]{1,2,0:T(8,128)(2,1)}), bf16[8,512,256]{1,2,0:T(8,128)(2,1)S(1)}, u32[]{:S(2)}, u32[]{:S(2)}) %all-to-all-start) | async-done | bytes 2097184 | tf_op jit(solution)/shard_map/all_to_all | solution.py:15
  35.9 2.1 stack.9
  37.9 10.5 %all-to-all-start.1 = ((bf16[32,64,768]{2,1,0:T(8,128)(2,1)}), bf16[32,64,768]{2,1,0:T(8,128)(2,1)}, u32[]{:S(2)}, u32[]{:S(2)}) async-start(bf16[32,64,768]{2,1,0:T(8,128)(2,1)} %stack.9), calls=%async_computation.1 | async-start | bytes 6291456 | tf_op jit(solution)/shard_map/all_to_all | solution.py:99
  49.9 1.9 fusion.2
  51.8 67.7 %all-to-all-done.1 = bf16[32,64,768]{2,1,0:T(8,128)(2,1)} async-done(((bf16[32,64,768]{2,1,0:T(8,128)(2,1)}), bf16[32,64,768]{2,1,0:T(8,128)(2,1)}, u32[]{:S(2)}, u32[]{:S(2)}) %all-to-all-start.1) | async-done | bytes 3145760 | tf_op jit(solution)/shard_map/all_to_all | solution.py:99
  119.4 1.1 broadcast_in_dim.39
  120.5 9.1 %all-to-all-start.2 = ((bf16[32,256,64]{1,2,0:T(8,128)(2,1)}), bf16[32,256,64]{1,2,0:T(8,128)(2,1)S(1)}, u32[]{:S(2)}, u32[]{:S(2)}) async-start(bf16[32,256,64]{1,2,0:T(8,128)(2,1)} %broadcast_in_dim.39), calls=%async_computation.2 | async-start | bytes 2097152 | tf_op jit(solution)/shard_map/all_to_all | solution.py:15
  129.6 4.6 convolution_convert_fusion.5
  134.3 1.4 copy.53
  136.1 1.6 fusion.253
  137.8 22.3 %all-gather.6 = bf16[8,2,128]{2,1,0:T(2,128)(2,1)S(1)} all-gather(bf16[1,2,128]{2,1,0:T(2,128)(2,1)S(1)} %bitcast.608), channel_id=3, replica_groups=mesh['seq_0'=4,'seq_1'=8,'grp'=8] {'seq_1'}, dimensions={0}, use_global_device_ids=true | all-gather | bytes 4608 | tf_op jit(solution)/shard_map/all_gather | solution.py:43
  160.0 7.5 %all_gather.65 = bf16[4,2,128]{2,1,0:T(2,128)(2,1)S(1)} all-gather(bf16[1,2,128]{2,1,0:T(2,128)(2,1)S(1)} %fusion.234), channel_id=1, replica_groups=mesh['seq_0'=4,'seq_1'=8,'grp'=8] {'seq_0'}, dimensions={0}, use_global_device_ids=true | all-gather | bytes 2560 | tf_op jit(solution)/shard_map/all_gather | solution.py:43
  168.2 19.6 %all-gather = bf16[16,128,128]{2,1,0:T(8,128)(2,1)S(1)} all-gather(bf16[2,128,128]{2,1,0:T(8,128)(2,1)S(1)} %convolution_convert_fusion.8), channel_id=2, replica_groups=mesh['seq_0'=4,'seq_1'=8,'grp'=8] {'seq_1'}, dimensions={0}, use_global_device_ids=true | all-gather | bytes 589824 | tf_op jit(solution)/shard_map/all_gather | solution.py:43
  187.9 9.4 %all_gather.62 = bf16[4,2,128,128]{3,2,1,0:T(8,128)(2,1)S(1)} all-gather(bf16[1,2,128,128]{3,2,1,0:T(8,128)(2,1)S(1)} %fusion.113), channel_id=1, replica_groups=mesh['seq_0'=4,'seq_1'=8,'grp'=8] {'seq_0'}, dimensions={0}, use_global_device_ids=true | all-gather | bytes 327680 | tf_op jit(solution)/shard_map/all_gather | solution.py:43
  197.3 1.6 fusion.38
  201.6 44.7 %all_to_all.60 = bf16[8,512,256]{2,1,0:T(8,128)(2,1)S(1)} all-to-all(bf16[8,512,256]{2,1,0:T(8,128)(2,1)S(1)} %bitcast.576), channel_id=1, replica_groups=mesh['seq_0'=4,'seq_1'=8,'grp'=8] {'grp'}, dimensions={0} | all-to-all | bytes 4194304 | tf_op jit(solution)/shard_map/all_to_all | solution.py:66
  247.7 30.0 %all_to_all.61 = bf16[8,512,256]{1,2,0:T(8,128)(2,1)S(1)} all-to-all(bf16[8,512,256]{1,2,0:T(8,128)(2,1)S(1)} %broadcast_in_dim.40), channel_id=1, replica_groups=mesh['seq_0'=4,'seq_1'=8,'grp'=8] {'grp'}, dimensions={0} | all-to-all | bytes 4194304 | tf_op jit(solution)/shard_map/all_to_all | solution.py:15
  277.6 2.1 stack.10
  279.7 6.7 all-to-all-start.5
  286.9 1.9 fusion.5
  288.8 68.5 %all-to-all-done.5 = bf16[32,64,768]{2,1,0:T(8,128)(2,1)} async-done(((bf16[32,64,768]{2,1,0:T(8,128)(2,1)}), bf16[32,64,768]{2,1,0:T(8,128)(2,1)}, u32[]{:S(2)}, u32[]{:S(2)}) %all-to-all-start.5) | async-done | bytes 3145760 | tf_op jit(solution)/shard_map/all_to_all | solution.py:99
  358.4 8.0 %all-to-all-start.6 = ((bf16[32,256,64]{1,2,0:T(8,128)(2,1)}), bf16[32,256,64]{1,2,0:T(8,128)(2,1)S(1)}, u32[]{:S(2)}, u32[]{:S(2)}) async-start(bf16[32,256,64]{1,2,0:T(8,128)(2,1)} %broadcast_in_dim.42), calls=%async_computation.6 | async-start | bytes 2097152 | tf_op jit(solution)/shard_map/all_to_all | solution.py:15
  366.4 4.4 convolution_convert_fusion.4
  371.5 1.6 fusion.254
  374.1 32.9 %all-gather.2 = bf16[16,128,128]{2,1,0:T(8,128)(2,1)S(1)} all-gather(bf16[2,128,128]{2,1,0:T(8,128)(2,1)S(1)} %convolution_convert_fusion.7), channel_id=4, replica_groups=mesh['seq_0'=4,'seq_1'=8,'grp'=8] {'seq_1'}, dimensions={0}, use_global_device_ids=true | all-gather | bytes 589824 | tf_op jit(solution)/shard_map/all_gather | solution.py:43
  407.5 10.2 %all-gather.7 = bf16[8,2,128]{2,1,0:T(2,128)(2,1)S(1)} all-gather(bf16[1,2,128]{2,1,0:T(2,128)(2,1)S(1)} %bitcast.606), channel_id=5, replica_groups=mesh['seq_0'=4,'seq_1'=8,'grp'=8] {'seq_1'}, dimensions={0}, use_global_device_ids=true | all-gather | bytes 4608 | tf_op jit(solution)/shard_map/all_gather | solution.py:43
  417.7 7.7 %all_gather.71 = bf16[4,2,128]{2,1,0:T(2,128)(2,1)S(1)} all-gather(bf16[1,2,128]{2,1,0:T(2,128)(2,1)S(1)} %fusion.235), channel_id=1, replica_groups=mesh['seq_0'=4,'seq_1'=8,'grp'=8] {'seq_0'}, dimensions={0}, use_global_device_ids=true | all-gather | bytes 2560 | tf_op jit(solution)/shard_map/all_gather | solution.py:43
  425.4 9.4 %all_gather.68 = bf16[4,2,128,128]{3,2,1,0:T(8,128)(2,1)S(1)} all-gather(bf16[1,2,128,128]{3,2,1,0:T(8,128)(2,1)S(1)} %fusion.112), channel_id=1, replica_groups=mesh['seq_0'=4,'seq_1'=8,'grp'=8] {'seq_0'}, dimensions={0}, use_global_device_ids=true | all-gather | bytes 327680 | tf_op jit(solution)/shard_map/all_gather | solution.py:43
  434.8 1.6 fusion.36
  436.7 1.6 select_reduce_fusion.1
  440.2 45.1 %all_to_all.62 = bf16[8,512,256]{2,1,0:T(8,128)(2,1)S(1)} all-to-all(bf16[8,512,256]{2,1,0:T(8,128)(2,1)S(1)} %bitcast.577), channel_id=1, replica_groups=mesh['seq_0'=4,'seq_1'=8,'grp'=8] {'grp'}, dimensions={0} | all-to-all | bytes 4194304 | tf_op jit(solution)/shard_map/all_to_all | solution.py:66
  486.0 30.0 %all_to_all.63 = bf16[8,512,256]{1,2,0:T(8,128)(2,1)S(1)} all-to-all(bf16[8,512,256]{1,2,0:T(8,128)(2,1)S(1)} %broadcast_in_dim.43), channel_id=1, replica_groups=mesh['seq_0'=4,'seq_1'=8,'grp'=8] {'grp'}, dimensions={0} | all-to-all | bytes 4194304 | tf_op jit(solution)/shard_map/all_to_all | solution.py:15
  515.9 2.1 stack.11
  518.0 7.1 all-to-all-start.9
  525.6 1.9 fusion.8
  527.5 68.7 %all-to-all-done.9 = bf16[32,64,768]{2,1,0:T(8,128)(2,1)} async-done(((bf16[32,64,768]{2,1,0:T(8,128)(2,1)}), bf16[32,64,768]{2,1,0:T(8,128)(2,1)}, u32[]{:S(2)}, u32[]{:S(2)}) %all-to-all-start.9) | async-done | bytes 3145760 | tf_op jit(solution)/shard_map/all_to_all | solution.py:99
  597.3 8.3 %all-to-all-start.10 = ((bf16[32,256,64]{1,2,0:T(8,128)(2,1)}), bf16[32,256,64]{1,2,0:T(8,128)(2,1)S(1)}, u32[]{:S(2)}, u32[]{:S(2)}) async-start(bf16[32,256,64]{1,2,0:T(8,128)(2,1)} %broadcast_in_dim.45), calls=%async_computation.10 | async-start | bytes 2097152 | tf_op jit(solution)/shard_map/all_to_all | solution.py:15
  605.6 4.4 convolution_convert_fusion.3
  610.7 1.6 fusion.255
  613.3 32.0 %all-gather.4 = bf16[16,128,128]{2,1,0:T(8,128)(2,1)S(1)} all-gather(bf16[2,128,128]{2,1,0:T(8,128)(2,1)S(1)} %convolution_convert_fusion.6), channel_id=6, replica_groups=mesh['seq_0'=4,'seq_1'=8,'grp'=8] {'seq_1'}, dimensions={0}, use_global_device_ids=true | all-gather | bytes 589824 | tf_op jit(solution)/shard_map/all_gather | solution.py:43
  645.8 11.0 %all-gather.8 = bf16[8,2,128]{2,1,0:T(2,128)(2,1)S(1)} all-gather(bf16[1,2,128]{2,1,0:T(2,128)(2,1)S(1)} %bitcast.607), channel_id=7, replica_groups=mesh['seq_0'=4,'seq_1'=8,'grp'=8] {'seq_1'}, dimensions={0}, use_global_device_ids=true | all-gather | bytes 4608 | tf_op jit(solution)/shard_map/all_gather | solution.py:43
  656.8 7.4 %all_gather.77 = bf16[4,2,128]{2,1,0:T(2,128)(2,1)S(1)} all-gather(bf16[1,2,128]{2,1,0:T(2,128)(2,1)S(1)} %fusion.236), channel_id=1, replica_groups=mesh['seq_0'=4,'seq_1'=8,'grp'=8] {'seq_0'}, dimensions={0}, use_global_device_ids=true | all-gather | bytes 2560 | tf_op jit(solution)/shard_map/all_gather | solution.py:43
  664.2 9.4 %all_gather.74 = bf16[4,2,128,128]{3,2,1,0:T(8,128)(2,1)S(1)} all-gather(bf16[1,2,128,128]{3,2,1,0:T(8,128)(2,1)S(1)} %fusion.111), channel_id=1, replica_groups=mesh['seq_0'=4,'seq_1'=8,'grp'=8] {'seq_0'}, dimensions={0}, use_global_device_ids=true | all-gather | bytes 327680 | tf_op jit(solution)/shard_map/all_gather | solution.py:43
  673.6 1.6 fusion.34
  675.4 1.5 select_reduce_fusion
  678.8 45.2 %all_to_all.64 = bf16[8,512,256]{2,1,0:T(8,128)(2,1)S(1)} all-to-all(bf16[8,512,256]{2,1,0:T(8,128)(2,1)S(1)} %bitcast.578), channel_id=1, replica_groups=mesh['seq_0'=4,'seq_1'=8,'grp'=8] {'grp'}, dimensions={0} | all-to-all | bytes 4194304 | tf_op jit(solution)/shard_map/all_to_all | solution.py:66
  (112 shorter events, 21.2 us)
Async XLA Ops:
  2.6 6.9 copy-start.2
  2.6 33.2 %all-to-all-start = ((bf16[8,512,256]{1,2,0:T(8,128)(2,1)}), bf16[8,512,256]{1,2,0:T(8,128)(2,1)S(1)}, u32[]{:S(2)}, u32[]{:S(2)}) async-start(bf16[8,512,256]{1,2,0:T(8,128)(2,1)} %broadcast_in_dim.37), calls=%async_computation | async-start | bytes 4194304 | tf_op jit(solution)/shard_map/all_to_all | solution.py:15
  37.9 10.5 %copy-start.9 = (f32[3,2048]{1,0:T(4,128)S(1)}, f32[3,2048]{1,0:T(4,128)}, u32[]{:S(2)}) copy-start(f32[3,2048]{1,0:T(4,128)} %param.10) | copy-start | bytes 73732
  37.9 11.4 %copy-start.10 = (f32[3,256]{1,0:T(4,128)S(1)}, f32[3,256]{1,0:T(4,128)}, u32[]{:S(2)}) copy-start(f32[3,256]{1,0:T(4,128)} %param.11) | copy-start | bytes 9220
  37.9 11.4 %copy-start.8 = (bf16[3,256,64]{1,2,0:T(8,128)(2,1)S(1)}, bf16[3,256,64]{1,2,0:T(8,128)(2,1)}, u32[]{:S(2)}) copy-start(bf16[3,256,64]{1,2,0:T(8,128)(2,1)} %param.8) | copy-start | bytes 294916
  37.9 81.5 %all-to-all-start.1 = ((bf16[32,64,768]{2,1,0:T(8,128)(2,1)}), bf16[32,64,768]{2,1,0:T(8,128)(2,1)}, u32[]{:S(2)}, u32[]{:S(2)}) async-start(bf16[32,64,768]{2,1,0:T(8,128)(2,1)} %stack.9), calls=%async_computation.1 | async-start | bytes 6291456 | tf_op jit(solution)/shard_map/all_to_all | solution.py:99
  51.8 77.9 %copy-start = (bf16[8,512,256]{1,2,0:T(8,128)(2,1)S(1)}, bf16[8,512,256]{1,2,0:T(8,128)(2,1)}, u32[]{:S(2)}) copy-start(bf16[8,512,256]{1,2,0:T(8,128)(2,1)} %fusion.2) | copy-start | bytes 6291460
  120.5 80.1 %all-to-all-start.2 = ((bf16[32,256,64]{1,2,0:T(8,128)(2,1)}), bf16[32,256,64]{1,2,0:T(8,128)(2,1)S(1)}, u32[]{:S(2)}, u32[]{:S(2)}) async-start(bf16[32,256,64]{1,2,0:T(8,128)(2,1)} %broadcast_in_dim.39), calls=%async_computation.2 | async-start | bytes 2097152 | tf_op jit(solution)/shard_map/all_to_all | solution.py:15
  137.7 61.4 %copy-start.3 = (pred[512,512]{0,1:T(8,128)(4,1)S(1)}, pred[512,512]{0,1:T(8,128)(4,1)}, u32[]{:S(2)}) copy-start(pred[512,512]{0,1:T(8,128)(4,1)} %iota_compare_fusion) | copy-start | bytes 786436
  246.3 1.0 copy-start.1
  279.7 77.6 %all-to-all-start.5 = ((bf16[32,64,768]{2,1,0:T(8,128)(2,1)}), bf16[32,64,768]{2,1,0:T(8,128)(2,1)}, u32[]{:S(2)}, u32[]{:S(2)}) async-start(bf16[32,64,768]{2,1,0:T(8,128)(2,1)} %stack.10), calls=%async_computation.5 | async-start | bytes 6291456 | tf_op jit(solution)/shard_map/all_to_all | solution.py:99
  358.4 80.9 %all-to-all-start.6 = ((bf16[32,256,64]{1,2,0:T(8,128)(2,1)}), bf16[32,256,64]{1,2,0:T(8,128)(2,1)S(1)}, u32[]{:S(2)}, u32[]{:S(2)}) async-start(bf16[32,256,64]{1,2,0:T(8,128)(2,1)} %broadcast_in_dim.42), calls=%async_computation.6 | async-start | bytes 2097152 | tf_op jit(solution)/shard_map/all_to_all | solution.py:15
  373.2 0.7 copy-start.6
  436.7 2.0 copy-start.4
  518.0 78.2 %all-to-all-start.9 = ((bf16[32,64,768]{2,1,0:T(8,128)(2,1)}), bf16[32,64,768]{2,1,0:T(8,128)(2,1)}, u32[]{:S(2)}, u32[]{:S(2)}) async-start(bf16[32,64,768]{2,1,0:T(8,128)(2,1)} %stack.11), calls=%async_computation.9 | async-start | bytes 6291456 | tf_op jit(solution)/shard_map/all_to_all | solution.py:99
  597.3 80.6 %all-to-all-start.10 = ((bf16[32,256,64]{1,2,0:T(8,128)(2,1)}), bf16[32,256,64]{1,2,0:T(8,128)(2,1)S(1)}, u32[]{:S(2)}, u32[]{:S(2)}) async-start(bf16[32,256,64]{1,2,0:T(8,128)(2,1)} %broadcast_in_dim.45), calls=%async_computation.10 | async-start | bytes 2097152 | tf_op jit(solution)/shard_map/all_to_all | solution.py:15
  612.3 0.7 copy-start.7
  612.3 63.1 %copy-start.5 = (pred[512,512]{0,1:T(8,128)(4,1)S(1)}, pred[512,512]{0,1:T(8,128)(4,1)}, u32[]{:S(2)}) copy-start(pred[512,512]{0,1:T(8,128)(4,1)} %iota_compare_fusion) | copy-start | bytes 786436
